TPU v7x, 32 devices: a whole 2x2x4 slice. The times are simulated.
32 devices in a mesh: groups: 2 (over x), ctx: 4 (over y, core), heads: 4 (over z).
Axes of the slice: x: 2, y: 2, z: 4, core: 2. Of those that a mesh axis runs over, the one named last changes fastest.
Arguments:
- tokens: bfloat16 [4096, 2048], P(('groups', 'ctx', 'heads')), parts along dimension 0, may hold values from -60 to 60
- state_in: float32 [4, 256, 128], P('heads', 'groups'), parts along dimension 1, may hold values from -256 to 256
- past_kv: bfloat16 [2, 1024, 512], P(None, 'groups', 'heads'), parts along dimension 1, may hold values from -6 to 6
- w_qkv: bfloat16 [2048, 3, 512], P(None, None, 'heads'), may hold values from -0.125 to 0.125
- w_out: bfloat16 [512, 2048], P('heads'), may hold values from -0.25 to 0.25
- w_gate: bfloat16 [16, 2048, 768], P(('ctx', 'heads')), may hold values from -0.125 to 0.125
- w_up: bfloat16 [16, 2048, 768], P(('ctx', 'heads')), may hold values from -0.125 to 0.125
- w_down: bfloat16 [16, 768, 2048], P(('ctx', 'heads')), may hold values from -0.21875 to 0.21875
- expert_ids: int32 [4096, 8], P(('groups', 'ctx', 'heads')), parts along dimension 0, may hold values from 0 to 15, all different within a row; in each aligned block of 128 rows (0 to 127, 128 to 255, ...) at most 128 rows name the same one
- gate_weights: float32 [4096, 8], P(('groups', 'ctx', 'heads')), parts along dimension 0, may hold values from 0.1 to 1
Outputs:
- mixed: bfloat16 [4096, 2048], P(('groups', 'ctx', 'heads')), parts along dimension 0
There are 2 independent parts, one for each index of `groups`. A program takes and returns all parts, laid end to end along the dimension named above; an argument that names none is the same for every part. Nothing has to cross between parts.
Inputs may be any that keep to these rules, and one draw needn't show every extreme that they name: `expert_ids`: each row names 8 different experts; in each aligned block of 128 rows (the rows of one device) no expert is named by more than 128 rows, a bound that some block reaches.
All inputs are finite; a program needn't handle non-finite values.
Results may differ from a plain program's by a relative error of at most 0.017.
Values may be sent and summed in bfloat16 or wider, within the bound.
A program may use at most 128 MiB of HBM per device.

v0:
```python
import math
import jax
import jax.numpy as jnp
from jax import lax
from jax.sharding import PartitionSpec as P

HDIM = 128
WINDOW = 512


def entering(x, axis, join, neutral):
    place = lax.axis_index(axis)
    gathered = lax.all_gather(x.astype(jnp.bfloat16), axis)
    state = jnp.zeros_like(x) + jnp.asarray(neutral, x.dtype)

    def one(lap, state):
        return join(state, lax.dynamic_index_in_dim(gathered, lap, 0, False).astype(x.dtype))

    return lax.fori_loop(0, place, one, state)


def from_behind(block, axis, distance):
    devices = range(lax.axis_size(axis))
    route = [(i - distance, i) for i in devices if i - distance in devices]
    return lax.ppermute(block, axis, route)


def normalize(value):
    return value * lax.rsqrt(jnp.mean(value * value, axis=-1, keepdims=True) + 1e-06)


def dense_experts(
    hidden_float, normed, w_gate, w_up, w_down, expert_ids, gate_weights, expert_count
):
    axes = ("ctx", "heads")
    exp_local = w_gate.shape[0]
    chosen = expert_ids[:, :, None] == jnp.arange(expert_count, dtype=jnp.int32)
    table = jnp.sum(jnp.where(chosen, gate_weights[:, :, None], 0.0), axis=1)
    weights = lax.all_gather(table, axes, axis=0, tiled=True)
    first = lax.axis_index(axes) * exp_local
    rows = lax.all_gather(normed, axes, axis=0, tiled=True)
    total = None
    for e in range(exp_local):
        gate_act = jnp.dot(rows, w_gate[e], preferred_element_type=jnp.float32)
        up_act = jnp.dot(rows, w_up[e], preferred_element_type=jnp.float32)
        hid = (jax.nn.silu(gate_act) * up_act).astype(jnp.bfloat16)
        out_rows = jnp.dot(hid, w_down[e], preferred_element_type=jnp.float32)
        weight = lax.dynamic_slice_in_dim(weights, first + e, 1, 1)
        part = weight * out_rows
        total = part if total is None else total + part
    routed = lax.psum_scatter(total.astype(jnp.bfloat16), axes, scatter_dimension=0, tiled=True)
    return (hidden_float + routed.astype(jnp.float32)).astype(jnp.bfloat16)


def on_device(
    tokens, state_in, past_kv, w_qkv, w_out, w_gate, w_up, w_down, expert_ids, gate_weights
):
    row_count, model_width = tokens.shape
    inner_width = w_qkv.shape[2]
    local_heads = inner_width // HDIM
    w_flat = w_qkv.reshape(model_width, 3 * inner_width)
    projected = jnp.dot(
        lax.all_gather(tokens, "heads", axis=0, tiled=True),
        w_flat,
        preferred_element_type=jnp.float32,
    ).astype(jnp.bfloat16)
    slab_rows = projected.shape[0]
    projected = projected.reshape(slab_rows, 3, local_heads, HDIM)
    query = jnp.transpose(projected[:, 0], (1, 0, 2))
    keys = jnp.transpose(projected[:, 1], (1, 0, 2))
    values = jnp.transpose(projected[:, 2], (1, 0, 2))
    local_state = jnp.einsum("hsd,hse->hde", keys, values, preferred_element_type=jnp.float32)
    earlier_state = entering(
        local_state, "ctx", lambda first, second: first + second, jnp.zeros_like(local_state)
    )
    start_state = state_in + earlier_state
    tail = jnp.stack([keys, values], axis=0)
    arrived = from_behind(tail, "ctx", 1)
    past = jnp.transpose(past_kv.reshape(2, WINDOW, local_heads, HDIM), (0, 2, 1, 3))
    previous = jnp.where(lax.axis_index("ctx") == 0, past, arrived)
    all_keys = jnp.concatenate([previous[0], keys], axis=1)
    all_values = jnp.concatenate([previous[1], values], axis=1)
    block_rows = min(slab_rows, 512)
    block_count = slab_rows // block_rows
    scale = 1.0 / math.sqrt(HDIM)
    causal = jnp.arange(block_rows)[:, None] >= jnp.arange(block_rows)[None, :]
    offsets = jnp.arange(WINDOW + block_rows)[None, :] - jnp.arange(block_rows)[:, None]
    in_window = (offsets > 0) & (offsets <= WINDOW)

    def block_step(state, index):
        first = index * block_rows
        carried = jnp.einsum(
            "hsd,hde->hse", query.astype(jnp.float32), state, precision=lax.Precision.HIGHEST
        )
        inside = jnp.einsum("hsd,htd->hst", query, keys, preferred_element_type=jnp.float32)
        inside = jnp.where(causal[None], inside, 0.0).astype(jnp.bfloat16)
        linear = carried + jnp.einsum(
            "hst,hte->hse", inside, values, preferred_element_type=jnp.float32
        )
        scores = (
            jnp.einsum("hsd,htd->hst", query, all_keys, preferred_element_type=jnp.float32) * scale
        )
        scores = jnp.where(in_window[None], scores, -jnp.inf)
        top_score = jnp.max(scores, axis=-1, keepdims=True)
        expo = jnp.exp(scores - top_score)
        probs = (expo / jnp.sum(expo, axis=-1, keepdims=True)).astype(jnp.bfloat16)
        window_out = jnp.einsum(
            "hst,hte->hse", probs, all_values, preferred_element_type=jnp.float32
        )
        combined = (normalize(linear) + window_out).astype(jnp.bfloat16)
        new_state = state + jnp.einsum(
            "hsd,hse->hde", keys, values, preferred_element_type=jnp.float32
        )
        return (new_state, combined)

    _, outs = lax.scan(block_step, start_state, jnp.arange(block_count, dtype=jnp.int32))
    heads_out = jnp.transpose(outs, (0, 2, 1, 3)).reshape(slab_rows, inner_width)
    regrouped = lax.all_to_all(heads_out, "heads", split_axis=0, concat_axis=1, tiled=True)
    attn = jnp.dot(
        regrouped,
        lax.all_gather(w_out, "heads", axis=0, tiled=True),
        preferred_element_type=jnp.float32,
    )
    hidden_state = (tokens.astype(jnp.float32) + attn).astype(jnp.bfloat16)
    hidden_float = hidden_state.astype(jnp.float32)
    normed = normalize(hidden_float).astype(jnp.bfloat16)
    ctx_count = lax.axis_size("ctx")
    head_count = lax.axis_size("heads")
    exp_local = w_gate.shape[0]
    expert_count = exp_local * ctx_count * head_count
    top_count = expert_ids.shape[1]
    capacity = max(2, 2 * row_count * top_count // expert_count)
    devices = ctx_count * head_count
    if row_count * devices <= expert_count * capacity:
        return dense_experts(
            hidden_float, normed, w_gate, w_up, w_down, expert_ids, gate_weights, expert_count
        )
    picks = expert_ids.reshape(-1)
    onehot = (picks[:, None] == jnp.arange(expert_count, dtype=jnp.int32)[None, :]).astype(
        jnp.int32
    )
    earlier = jnp.cumsum(onehot, axis=0) - onehot
    slots = jnp.sum(onehot * earlier, axis=1)
    destination = picks * capacity + slots
    source_rows = jnp.arange(row_count * top_count, dtype=jnp.int32) // top_count
    outgoing = jnp.zeros((expert_count * capacity, model_width), jnp.bfloat16)
    outgoing = outgoing.at[destination].set(normed[source_rows])
    sendable = outgoing.reshape(expert_count, 1, capacity, model_width)
    arrived_rows = lax.all_to_all(
        sendable, ("ctx", "heads"), split_axis=0, concat_axis=1, tiled=True
    )
    e_count, n_count, c_count, d_count = arrived_rows.shape
    flat = arrived_rows.reshape(e_count, n_count * c_count, d_count)
    gate_act = jnp.einsum("erd,edf->erf", flat, w_gate, preferred_element_type=jnp.float32)
    up_act = jnp.einsum("erd,edf->erf", flat, w_up, preferred_element_type=jnp.float32)
    hid = (jax.nn.silu(gate_act) * up_act).astype(jnp.bfloat16)
    out_rows = jnp.einsum("erf,efd->erd", hid, w_down, preferred_element_type=jnp.float32)
    finished = out_rows.astype(jnp.bfloat16).reshape(e_count, n_count, c_count, d_count)
    returned = lax.all_to_all(finished, ("ctx", "heads"), split_axis=1, concat_axis=0, tiled=True)
    returned = returned.reshape(expert_count * capacity, model_width)
    picked = returned[destination].reshape(row_count, top_count, model_width).astype(jnp.float32)
    routed = jnp.sum(gate_weights[:, :, None] * picked, axis=1)
    return (hidden_float + routed).astype(jnp.bfloat16)


def solution(mesh):
    return jax.shard_map(
        on_device,
        mesh=mesh,
        in_specs=(
            P(("groups", "ctx", "heads"), None),
            P("heads", "groups", None),
            P(None, "groups", "heads"),
            P(None, None, "heads"),
            P("heads", None),
            P(("ctx", "heads"), None, None),
            P(("ctx", "heads"), None, None),
            P(("ctx", "heads"), None, None),
            P(("groups", "ctx", "heads"), None),
            P(("groups", "ctx", "heads"), None),
        ),
        out_specs=P(("groups", "ctx", "heads"), None),
        check_vma=False,
    )
```

profile of v0, /device:TPU:0, one launch (start us, length us, event | category | flops | bytes accessed | tf_op | source)
XLA Modules:
  0.0 328.5 jit_solution(8045174008604358506)
XLA Ops:
  6.5 0.0 copy-start
  6.5 0.0 all-gather.5.cloned.1.call-start
  6.5 0.7 all-gather.5.cloned.1.call-update
  7.3 0.0 all-gather.7.cloned.1.call-start
  7.3 0.7 all-gather.7.cloned.1.call-update
  8.0 2.6 copy.27
  10.6 46.7 %all-gather.5.cloned.1.call-done = bf16[512,2048]{1,0:T(8,128)(2,1)} async-done(((bf16[128,2048]{1,0:T(8,128)(2,1)}), bf16[512,2048]{1,0:T(8,128)(2,1)}) %all-gather.5.cloned.1.call-update) | async-done | bytes 2097168 | tf_op jit(solution)/shard_map/all_gather | solution.py:63
  57.3 3.1 convolution_convert_fusion
  60.4 0.0 copy-start.3
  60.4 0.2 convolution_convert_fusion.1
  60.6 0.7 fusion.38
  61.3 5.4 %all-gather = bf16[512,128]{1,0:T(8,128)(2,1)S(1)} all-gather(bf16[128,128]{1,0:T(8,128)(2,1)S(1)} %convolution_convert_fusion.1), channel_id=2, replica_groups=mesh['groups'=2,'ctx'=4,'heads'=4] {'ctx'}, dimensions={0}, use_global_device_ids=true | all-gather | bytes 163840 | tf_op jit(solution)/shard_map/all_gather | solution.py:13
  66.7 0.0 copy-done.3
  66.7 1.0 copy.35
  67.8 1.7 copy.34
  69.4 1.6 pad_maximum_fusion
  71.1 3.0 collective-permute-start
  74.0 0.0 copy-done.4
  74.0 2.0 fusion.26
  76.0 2.3 multiply_reduce_fusion.1
  78.3 0.0 collective-permute-done
  78.3 1.1 bitcast_select_fusion
  79.4 0.0 copy-done.2
  79.4 0.0 copy-start.7
  79.4 1.5 fusion.39
  80.9 0.5 fusion.11
  81.5 0.0 copy-done.7
  81.5 0.6 fusion.15
  82.1 0.8 copy.33
  82.8 3.5 %all-to-all-start = ((bf16[4,128,128]{1,2,0:T(8,128)(2,1)}), bf16[4,128,128]{1,2,0:T(8,128)(2,1)S(1)}, u32[]{:S(2)}, u32[]{:S(2)}) async-start(bf16[4,128,128]{1,2,0:T(8,128)(2,1)} %copy.33), calls=%async_computation | async-start | bytes 262144 | tf_op jit(solution)/shard_map/all_to_all | solution.py:118
  86.3 0.0 all-gather.9.cloned.1.call-start
  86.3 19.8 %all-gather.7.cloned.1.call-done = bf16[512,2048]{1,0:T(8,128)(2,1)} async-done(((bf16[128,2048]{1,0:T(8,128)(2,1)}), bf16[512,2048]{1,0:T(8,128)(2,1)}) %all-gather.7.cloned.1.call-update) | async-done | bytes 2097168 | tf_op jit(solution)/shard_map/all_gather | solution.py:121
  106.2 0.0 all-to-all-done
  106.2 2.2 multiply_reduce_fusion
  108.4 0.0 copy-start.1
  108.4 1.0 copy-done.1
  109.4 0.9 multiply_convert_fusion.2
  110.3 0.0 all-gather.9.cloned.1.call-update
  110.4 0.0 reduce-scatter.2.cloned.1.call-start
  110.4 0.0 copy-done.5
  110.5 33.1 %all_gather.22 = f32[2048,16]{0,1:T(8,128)S(1)} all-gather(f32[128,16]{0,1:T(8,128)S(1)} %select_reduce_fusion), channel_id=1, replica_groups=mesh['groups'=2,'ctx'=4,'heads'=4] {'ctx','heads'}, dimensions={0}, use_global_device_ids=true | all-gather | bytes 139264 | tf_op jit(solution)/shard_map/all_gather | solution.py:39
  143.6 41.7 %all-gather.9.cloned.1.call-done = bf16[2048,2048]{1,0:T(8,128)(2,1)} async-done(((bf16[128,2048]{1,0:T(8,128)(2,1)}), bf16[2048,2048]{1,0:T(8,128)(2,1)}) %all-gather.9.cloned.1.call-update) | async-done | bytes 8388624 | tf_op jit(solution)/shard_map/all_gather | solution.py:41
  185.3 11.7 %fusion.3 = f32[2048,768]{1,0:T(8,128)} fusion(bf16[2048,2048]{1,0:T(8,128)(2,1)} %all-gather.9.cloned.1.call-done, bf16[1,2048,768]{2,1,0:T(8,128)(2,1)} %param.17), kind=kOutput, calls=%fused_computation.5 | convolution fusion | flops 6442450944 | bytes 17825792 | tf_op jit(solution)/shard_map/dot_general | solution.py:44
  197.0 0.0 copy-done
  197.0 20.6 %multiply_convert_fusion = bf16[2048,2048]{1,0:T(8,128)(2,1)} fusion(f32[2048]{0:T(1024)S(1)} %bitcast.98, f32[2048,768]{1,0:T(8,128)} %fusion.3, bf16[2048,2048]{1,0:T(8,128)(2,1)} %all-gather.9.cloned.1.call-done, bf16[1,768,2048]{2,1,0:T(8,128)(2,1)S(1)} %copy-done, bf16[1,2048,768]{2,1,0:T(8,128)(2,1)} %param.18), kind=kOutput, calls=%fused_computation.1 | convolution fusion | flops 12902727680 | bytes 29368320 | tf_op jit(solution)/shard_map/dot_general | solution.py:47
  217.5 0.0 reduce-scatter.2.cloned.1.call-update
  217.6 102.2 %reduce-scatter.2.cloned.1.call-done = bf16[128,2048]{1,0:T(8,128)(2,1)} async-done(((bf16[2048,2048]{1,0:T(8,128)(2,1)}), bf16[128,2048]{1,0:T(8,128)(2,1)}) %reduce-scatter.2.cloned.1.call-update) | async-done | bytes 524304 | tf_op jit(solution)/shard_map/reduce_scatter | solution.py:51
  319.7 2.3 add_convert_fusion
  (13 shorter events, 0.1 us)
Async XLA Ops:
  6.5 190.4 %copy-start = (bf16[1,768,2048]{2,1,0:T(8,128)(2,1)S(1)}, bf16[1,768,2048]{2,1,0:T(8,128)(2,1)}, u32[]{:S(2)}) copy-start(bf16[1,768,2048]{2,1,0:T(8,128)(2,1)} %param.19) | copy-start | bytes 9437188
  6.5 50.8 %all-gather.5.cloned.1.call-start = ((), (), s32[]{:S(2)}) async-start(), calls=%async_computation.2 | async-start | bytes 2621440 | tf_op jit(solution)/shard_map/all_gather | solution.py:63
  7.3 98.9 %all-gather.7.cloned.1.call-start = ((), (), s32[]{:S(2)}) async-start(), calls=%async_computation.3 | async-start | bytes 2621440 | tf_op jit(solution)/shard_map/all_gather | solution.py:121
  57.3 16.7 %copy-start.4 = (f32[1,128,128]{2,1,0:T(8,128)S(1)}, f32[1,128,128]{2,1,0:T(8,128)}, u32[]{:S(2)}) copy-start(f32[1,128,128]{2,1,0:T(8,128)} %param.13) | copy-start | bytes 196612
  60.4 6.3 %copy-start.3 = (bf16[512,384]{0,1:T(8,128)(2,1)}, bf16[512,384]{0,1:T(8,128)(2,1)S(1)}, u32[]{:S(2)}) copy-start(bf16[512,384]{0,1:T(8,128)(2,1)S(1)} %convolution_convert_fusion) | copy-start | bytes 1179652
  71.1 7.3 %collective-permute-start = (bf16[2,1,512,128]{3,2,1,0:T(8,128)(2,1)}, bf16[2,1,512,128]{3,2,1,0:T(8,128)(2,1)}, u32[]{:S(2)}, u32[]{:S(2)}) collective-permute-start(bf16[2,1,512,128]{3,2,1,0:T(8,128)(2,1)} %pad_maximum_fusion), channel_id=1, source_target_pairs={{0,4},{4,8},{8,12},{1,5},{5,9},{9,13},{2,6},{6,10},{10,14},{3,7},{... | collective-permute-start | bytes 786440 | tf_op jit(solution)/shard_map/ppermute | solution.py:25
  74.0 5.4 %copy-start.2 = (bf16[512,1,1,128]{3,0,2,1:T(8,128)(2,1)S(1)}, bf16[512,1,1,128]{3,0,2,1:T(8,128)(2,1)}, u32[]{:S(2)}) copy-start(bf16[512,1,1,128]{3,0,2,1:T(8,128)(2,1)} %copy.34) | copy-start | bytes 393220
  79.4 2.1 copy-start.7
  82.8 27.6 %copy-start.5 = (f32[128,8]{0,1:T(8,128)S(1)}, f32[128,8]{0,1:T(8,128)}, u32[]{:S(2)}) copy-start(f32[128,8]{0,1:T(8,128)} %param.21) | copy-start | bytes 12292
  82.8 27.6 %copy-start.6 = (s32[128,8]{0,1:T(8,128)S(1)}, s32[128,8]{0,1:T(8,128)}, u32[]{:S(2)}) copy-start(s32[128,8]{0,1:T(8,128)} %param.20) | copy-start | bytes 12292
  82.8 23.4 %all-to-all-start = ((bf16[4,128,128]{1,2,0:T(8,128)(2,1)}), bf16[4,128,128]{1,2,0:T(8,128)(2,1)S(1)}, u32[]{:S(2)}, u32[]{:S(2)}) async-start(bf16[4,128,128]{1,2,0:T(8,128)(2,1)} %copy.33), calls=%async_computation | async-start | bytes 262144 | tf_op jit(solution)/shard_map/all_to_all | solution.py:118
  86.3 99.0 %all-gather.9.cloned.1.call-start = ((), (), s32[]{:S(2)}) async-start(), calls=%async_computation.4 | async-start | bytes 8912896 | tf_op jit(solution)/shard_map/all_gather | solution.py:41
  108.4 1.0 copy-start.1
  110.4 209.4 %reduce-scatter.2.cloned.1.call-start = ((), (), s32[]{:S(2)}) async-start(), calls=%async_computation.5 | async-start | bytes 8912896 | tf_op jit(solution)/shard_map/reduce_scatter | solution.py:51
Sparse Core Ops, SparseCore 0:
  8.9 48.3 all-gather.4
  58.9 47.2 all-gather.6
  110.5 74.7 all-gather.8
  217.7 101.9 reduce-scatter.1
where the time goes:
time: 329 us
  waiting for transfers between devices  212 us (64%)
  matrix products  44.1 us (13%)
  blocking collectives  38.5 us (12%)
  between operations  13.3 us (4%)
  local copies, waits for them, and re-layouts  7.86 us (2%)
  starting transfers between devices  6.54 us (2%)
  other arithmetic  6.41 us (2%)
    reduce_scatter x1, waiting for transfers between devices, dense_experts(): lax.psum_scatter(total.astype(jnp.bfloat16), axes, scatter_dimension=0, t...  102 us
    all_gather x1, waiting for transfers between devices, on_device(): lax.all_gather(tokens, 'heads', axis=0, tiled=True)  46.7 us
    all_gather x1, waiting for transfers between devices, dense_experts(): rows = lax.all_gather(normed, axes, axis=0, tiled=True)  41.7 us
    all_gather x1, blocking collectives, dense_experts(): weights = lax.all_gather(table, axes, axis=0, tiled=True)  33.1 us
    dot_general x1, matrix products, dense_experts(): out_rows = jnp.dot(hid, w_down[e], preferred_element_type=jnp.float32)  20.6 us
    all_gather x1, waiting for transfers between devices, on_device(): lax.all_gather(w_out, 'heads', axis=0, tiled=True)  19.8 us
    dot_general x1, matrix products, dense_experts(): gate_act = jnp.dot(rows, w_gate[e], preferred_element_type=jnp.float32)  11.7 us
  transfers between devices with their start and end apart: 6, of which 4 were waited for; matrix products, arithmetic and copies ran while one was open for 6% of the time, Pallas kernels for 0%

commit v1 on v0

--- a/solution.py
+++ b/solution.py
@@ -36,9 +36,12 @@
     exp_local = w_gate.shape[0]
     chosen = expert_ids[:, :, None] == jnp.arange(expert_count, dtype=jnp.int32)
     table = jnp.sum(jnp.where(chosen, gate_weights[:, :, None], 0.0), axis=1)
-    weights = lax.all_gather(table, axes, axis=0, tiled=True)
     first = lax.axis_index(axes) * exp_local
-    rows = lax.all_gather(normed, axes, axis=0, tiled=True)
+    weights, rows = jnp.split(
+        lax.all_gather(jnp.concatenate([table, normed], axis=1), axes, axis=0, tiled=True),
+        [table.shape[1]],
+        axis=1,
+    )
     total = None
     for e in range(exp_local):
         gate_act = jnp.dot(rows, w_gate[e], preferred_element_type=jnp.float32)

time: 329 us -> 359 us (1.091)
  waiting for transfers between devices: 212 us -> 269 us
  blocking collectives: 38.5 us -> 5.4 us
    all_gather x1, waiting for transfers between devices: 41.7 us -> 97.5 us  [dense_experts(): lax.all_gather(jnp.concatenate([table, normed], axis=1), axes, axis=0, ti...]
    all_gather x1 -> x0, blocking collectives: 33.1 us -> none  [dense_experts(): weights = lax.all_gather(table, axes, axis=0, tiled=True)]
where the time goes in v1:
time: 359 us; the launch traced here: 358 us
  waiting for transfers between devices  269 us (75%)
  matrix products  46.8 us (13%)
  between operations  13.3 us (4%)
  local copies, waits for them, and re-layouts  10.2 us (3%)
  other arithmetic  7.02 us (2%)
  starting transfers between devices  6.58 us (2%)
  blocking collectives  5.4 us (2%)
    reduce_scatter x1, waiting for transfers between devices, dense_experts(): lax.psum_scatter(total.astype(jnp.bfloat16), axes, scatter_dimension=0, t...  104 us
    all_gather x1, waiting for transfers between devices, dense_experts(): lax.all_gather(jnp.concatenate([table, normed], axis=1), axes, axis=0, ti...  97.5 us
    all_gather x1, waiting for transfers between devices, on_device(): lax.all_gather(tokens, 'heads', axis=0, tiled=True)  46.7 us
    dot_general x1, matrix products, dense_experts(): out_rows = jnp.dot(hid, w_down[e], preferred_element_type=jnp.float32)  22.7 us
    all_gather x1, waiting for transfers between devices, on_device(): lax.all_gather(w_out, 'heads', axis=0, tiled=True)  19.8 us
    dot_general x1, matrix products, dense_experts(): gate_act = jnp.dot(rows, w_gate[e], preferred_element_type=jnp.float32)  12.2 us
  transfers between devices with their start and end apart: 6, of which 4 were waited for; matrix products, arithmetic and copies ran while one was open for 6% of the time, Pallas kernels for 0%

profile of v1, /device:TPU:0, one launch (start us, length us, event | category | flops | bytes accessed | tf_op | source)
XLA Modules:
  0.0 358.2 jit_solution(7078707776119002102)
XLA Ops:
  6.5 0.0 copy-start
  6.5 0.0 all-gather.5.cloned.1.call-start
  6.5 0.7 all-gather.5.cloned.1.call-update
  7.3 0.0 all-gather.7.cloned.1.call-start
  7.3 0.7 all-gather.7.cloned.1.call-update
  8.0 2.6 copy.27
  10.6 46.7 %all-gather.5.cloned.1.call-done = bf16[512,2048]{1,0:T(8,128)(2,1)} async-done(((bf16[128,2048]{1,0:T(8,128)(2,1)}), bf16[512,2048]{1,0:T(8,128)(2,1)}) %all-gather.5.cloned.1.call-update) | async-done | bytes 2097168 | tf_op jit(solution)/shard_map/all_gather | solution.py:66
  57.3 3.1 convolution_convert_fusion
  60.4 0.0 copy-start.3
  60.4 0.2 convolution_convert_fusion.1
  60.6 0.7 fusion.46
  61.3 5.4 %all-gather = bf16[512,128]{1,0:T(8,128)(2,1)S(1)} all-gather(bf16[128,128]{1,0:T(8,128)(2,1)S(1)} %convolution_convert_fusion.1), channel_id=2, replica_groups=mesh['groups'=2,'ctx'=4,'heads'=4] {'ctx'}, dimensions={0}, use_global_device_ids=true | all-gather | bytes 163840 | tf_op jit(solution)/shard_map/all_gather | solution.py:13
  66.7 0.0 copy-done.3
  66.7 1.0 copy.36
  67.8 1.7 copy.35
  69.4 1.6 pad_maximum_fusion.1
  71.1 2.9 collective-permute-start
  74.0 0.0 copy-done.4
  74.0 2.0 fusion.34
  76.0 2.3 multiply_reduce_fusion.1
  78.3 0.0 collective-permute-done
  78.3 1.1 bitcast_select_fusion
  79.4 1.5 fusion.47
  81.0 0.5 fusion.18
  81.5 0.0 copy-start.5
  81.5 0.0 copy-start.6
  81.5 0.6 fusion.22
  82.1 0.8 copy.33
  82.9 3.3 all-to-all-start
  86.2 0.0 all-gather.9.cloned.1.call-start
  86.3 0.1 copy.34
  86.4 19.8 %all-gather.7.cloned.1.call-done = bf16[512,2048]{1,0:T(8,128)(2,1)} async-done(((bf16[128,2048]{1,0:T(8,128)(2,1)}), bf16[512,2048]{1,0:T(8,128)(2,1)}) %all-gather.7.cloned.1.call-update) | async-done | bytes 2097168 | tf_op jit(solution)/shard_map/all_gather | solution.py:124
  106.2 0.0 all-to-all-done
  106.2 2.2 multiply_reduce_fusion
  108.4 1.0 copy-done.1
  109.4 0.1 fusion.23
  109.5 1.4 pad_maximum_fusion
  110.9 0.0 all-gather.9.cloned.1.call-update
  111.0 0.2 reduce-scatter.2.cloned.1.call-start
  111.2 97.5 %all-gather.9.cloned.1.call-done = f32[2048,2064]{1,0:T(8,128)} async-done(((f32[128,2064]{1,0:T(8,128)}), f32[2048,2064]{1,0:T(8,128)}) %all-gather.9.cloned.1.call-update) | async-done | bytes 16908304 | tf_op jit(solution)/shard_map/all_gather | solution.py:41
  208.7 1.4 split.8
  210.1 0.6 dynamic-slice_reduce_fusion
  210.7 0.1 copy-done.7
  210.9 12.2 %fusion.2 = f32[2048,768]{1,0:T(8,128)} fusion(f32[2048,2064]{1,0:T(8,128)} %all-gather.9.cloned.1.call-done, bf16[1,2048,768]{2,1,0:T(8,128)(2,1)S(1)} %copy-done.7), kind=kOutput, calls=%fused_computation.4 | convolution fusion | flops 6442450944 | bytes 17825792 | tf_op jit(solution)/shard_map/dot_general | solution.py:47
  223.1 22.7 %multiply_convert_fusion = bf16[2048,2048]{1,0:T(8,128)(2,1)} fusion(f32[2048]{0:T(1024)S(1)} %dynamic-slice_reduce_fusion, f32[2048,768]{1,0:T(8,128)} %fusion.2, f32[2048,2064]{1,0:T(8,128)} %all-gather.9.cloned.1.call-done, bf16[1,768,2048]{2,1,0:T(8,128)(2,1)S(1)} %copy-done, bf16[1,2048,768]{2,1,0:T(8,128)(2,1)} %param.18), kind=kOutput, calls=%fused_computation.1 | convolution fusion | flops 12902727680 | bytes 29368320 | tf_op jit(solution)/shard_map/dot_general | solution.py:50
  245.8 0.0 reduce-scatter.2.cloned.1.call-update
  245.8 103.6 %reduce-scatter.2.cloned.1.call-done = bf16[128,2048]{1,0:T(8,128)(2,1)} async-done(((bf16[2048,2048]{1,0:T(8,128)(2,1)}), bf16[128,2048]{1,0:T(8,128)(2,1)}) %reduce-scatter.2.cloned.1.call-update) | async-done | bytes 524304 | tf_op jit(solution)/shard_map/reduce_scatter | solution.py:54
  349.4 2.3 add_convert_fusion
  (17 shorter events, 0.1 us)
Async XLA Ops:
  6.5 216.6 %copy-start = (bf16[1,768,2048]{2,1,0:T(8,128)(2,1)S(1)}, bf16[1,768,2048]{2,1,0:T(8,128)(2,1)}, u32[]{:S(2)}) copy-start(bf16[1,768,2048]{2,1,0:T(8,128)(2,1)} %param.19) | copy-start | bytes 9437188
  6.5 50.8 %all-gather.5.cloned.1.call-start = ((), (), s32[]{:S(2)}) async-start(), calls=%async_computation.2 | async-start | bytes 2621440 | tf_op jit(solution)/shard_map/all_gather | solution.py:66
  7.3 98.9 %all-gather.7.cloned.1.call-start = ((), (), s32[]{:S(2)}) async-start(), calls=%async_computation.3 | async-start | bytes 2621440 | tf_op jit(solution)/shard_map/all_gather | solution.py:124
  57.3 16.7 %copy-start.4 = (f32[1,128,128]{2,1,0:T(8,128)S(1)}, f32[1,128,128]{2,1,0:T(8,128)}, u32[]{:S(2)}) copy-start(f32[1,128,128]{2,1,0:T(8,128)} %param.13) | copy-start | bytes 196612
  60.4 6.3 %copy-start.3 = (bf16[512,384]{0,1:T(8,128)(2,1)}, bf16[512,384]{0,1:T(8,128)(2,1)S(1)}, u32[]{:S(2)}) copy-start(bf16[512,384]{0,1:T(8,128)(2,1)S(1)} %convolution_convert_fusion) | copy-start | bytes 1179652
  71.1 7.3 %collective-permute-start = (bf16[2,1,512,128]{3,2,1,0:T(8,128)(2,1)}, bf16[2,1,512,128]{3,2,1,0:T(8,128)(2,1)}, u32[]{:S(2)}, u32[]{:S(2)}) collective-permute-start(bf16[2,1,512,128]{3,2,1,0:T(8,128)(2,1)} %pad_maximum_fusion.1), channel_id=1, source_target_pairs={{0,4},{4,8},{8,12},{1,5},{5,9},{9,13},{2,6},{6,10},{10,14},{3,7},{... | collective-permute-start | bytes 786440 | tf_op jit(solution)/shard_map/ppermute | solution.py:25
  74.0 5.4 %copy-start.2 = (bf16[512,1,1,128]{3,0,2,1:T(8,128)(2,1)S(1)}, bf16[512,1,1,128]{3,0,2,1:T(8,128)(2,1)}, u32[]{:S(2)}) copy-start(bf16[512,1,1,128]{3,0,2,1:T(8,128)(2,1)} %copy.35) | copy-start | bytes 393220
  79.4 2.1 copy-start.8
  81.5 4.8 %copy-start.5 = (f32[128,8]{0,1:T(8,128)S(1)}, f32[128,8]{0,1:T(8,128)}, u32[]{:S(2)}) copy-start(f32[128,8]{0,1:T(8,128)} %param.21) | copy-start | bytes 12292
  81.5 4.8 %copy-start.6 = (s32[128,8]{0,1:T(8,128)S(1)}, s32[128,8]{0,1:T(8,128)}, u32[]{:S(2)}) copy-start(s32[128,8]{0,1:T(8,128)} %param.20) | copy-start | bytes 12292
  82.9 23.3 %all-to-all-start = ((bf16[4,128,128]{1,2,0:T(8,128)(2,1)}), bf16[4,128,128]{1,2,0:T(8,128)(2,1)S(1)}, u32[]{:S(2)}, u32[]{:S(2)}) async-start(bf16[4,128,128]{1,2,0:T(8,128)(2,1)} %copy.33), calls=%async_computation | async-start | bytes 262144 | tf_op jit(solution)/shard_map/all_to_all | solution.py:121
  86.2 122.4 %all-gather.9.cloned.1.call-start = ((), (), s32[]{:S(2)}) async-start(), calls=%async_computation.4 | async-start | bytes 18939904 | tf_op jit(solution)/shard_map/all_gather | solution.py:41
  108.4 1.0 copy-start.1
  111.0 238.5 %reduce-scatter.2.cloned.1.call-start = ((), (), s32[]{:S(2)}) async-start(), calls=%async_computation.5 | async-start | bytes 8912896 | tf_op jit(solution)/shard_map/reduce_scatter | solution.py:54
  208.7 2.2 copy-start.7
Sparse Core Ops, SparseCore 0:
  8.9 48.3 all-gather.4
  58.9 47.2 all-gather.6
  111.1 97.5 all-gather.8
  245.9 103.4 reduce-scatter.1
